TPU v7x, 512 devices: a whole 4x8x8 slice. The times are simulated.
512 devices in a mesh: fsdp: 32 (over y, x_hi, core), tensor: 16 (over x_lo, z).
Axes of the slice: x: 4 (x_hi: 2, x_lo: 2; x = x_hi * 2 + x_lo), y: 8, z: 8, core: 2. Of those that a mesh axis runs over, the one named last changes fastest.
Arguments:
- out_grad: bfloat16 [4096, 8192], P(('fsdp', 'tensor')), may hold values from -24 to 24
- live_rows: int32 [512], P(('fsdp', 'tensor')), may hold values from 1 to 8, as said below
- gate_pre: bfloat16 [4096, 12288], P('fsdp', 'tensor'), may hold values from -8 to 8
- up_pre: bfloat16 [4096, 12288], P('fsdp', 'tensor'), may hold values from -6 to 6
- down_weight: bfloat16 [12288, 8192], P('tensor', 'fsdp'), may hold values from -0.15625 to 0.15625
- tile_mask: int32 [96, 64], P('tensor'), may hold values from 0 to 1, as said below
Outputs:
- d_gate: bfloat16 [4096, 12288], P('fsdp', 'tensor')
- d_up: bfloat16 [4096, 12288], P('fsdp', 'tensor')
- d_weight: bfloat16 [12288, 8192], P('tensor', 'fsdp')
Inputs may be any that keep to these rules, and one draw needn't show every extreme that they name: `tile_mask`: each device's shard of 6 x 2 tiles holds 1 to 4 kept tiles; in every draw the shards of some tensor index all hold exactly 4, and every tensor index has a shard holding 4. `live_rows`: some device has all 8 rows live in every draw.
All inputs are finite; a program needn't handle non-finite values.
Results may differ from a plain program's by a relative error of at most 0.015.
Values may be sent and summed in bfloat16 or wider, within the bound.
No kernel may reach another device: no remote copies, remote signals or barrier semaphores. Data moves between devices by JAX's collectives and lax.ppermute only.
A program may use at most 64 MiB of HBM per device.

v0:
```python
import math
import jax
import jax.numpy as jnp
from jax import lax
from jax.sharding import PartitionSpec as P

BLK = 128
CAP = 4


def split_count(slot_count):
    group_size = CAP * math.gcd(slot_count // CAP, 8)
    return (group_size, slot_count // group_size)


def per_device(out_grad, live_rows, gate_pre, up_pre, down_weight, tile_mask):
    fsdp_count = lax.axis_size("fsdp")
    fsdp_index = lax.axis_index("fsdp")
    tok_rows = out_grad.shape[0]
    row_blocks = tile_mask.shape[0]
    col_blocks = down_weight.shape[1] // BLK
    local_count = row_blocks * col_blocks
    live_mask = jnp.arange(tok_rows)[:, None] < live_rows[0]
    masked_grad = jnp.where(live_mask, out_grad, jnp.zeros_like(out_grad))
    grad_panel = lax.all_gather(masked_grad, "tensor", axis=0, tiled=True)
    rows_all = grad_panel.shape[0]
    panel_tiles = grad_panel.reshape(rows_all, fsdp_count * col_blocks, BLK)
    shard_masks = (
        tile_mask.reshape(row_blocks, fsdp_count, col_blocks)
        .transpose(1, 0, 2)
        .reshape(fsdp_count, local_count)
    )
    position = jnp.cumsum(shard_masks, axis=1) - 1
    chosen = (shard_masks[:, None, :] == 1) & (
        position[:, None, :] == jnp.arange(CAP)[None, :, None]
    )
    chosen_int = chosen.astype(jnp.int32)
    block_id = jnp.sum(chosen_int * jnp.arange(local_count)[None, None, :], axis=2)
    occupied = jnp.sum(chosen_int, axis=2)
    tile_row = (block_id // col_blocks).reshape(-1)
    tile_col = (jnp.arange(fsdp_count)[:, None] * col_blocks + block_id % col_blocks).reshape(-1)
    tile_live = occupied.reshape(-1).astype(jnp.float32)
    own_choice = lax.dynamic_index_in_dim(chosen_int, fsdp_index, 0, keepdims=False)
    local_tiles = (
        down_weight.reshape(row_blocks, BLK, col_blocks, BLK)
        .transpose(0, 2, 1, 3)
        .reshape(local_count, BLK, BLK)
    )
    packed = jnp.einsum(
        "sb,bij->sij",
        own_choice.astype(jnp.bfloat16),
        local_tiles,
        preferred_element_type=jnp.float32,
    ).astype(jnp.bfloat16)
    gate_value = gate_pre.astype(jnp.float32)
    up_value = up_pre.astype(jnp.float32)
    sigmoid_gate = jax.nn.sigmoid(gate_value)
    hidden = (gate_value * sigmoid_gate * up_value).astype(jnp.bfloat16)
    hidden_tiles = hidden.reshape(rows_all, row_blocks, BLK)
    grad_scale = 1.0 / math.sqrt(rows_all * fsdp_count)
    row_ids = jnp.arange(row_blocks)
    start_sum = jnp.zeros((rows_all, row_blocks, BLK), jnp.float32)
    running_sum = start_sum
    shard_piece = lax.all_gather(packed, "fsdp", axis=0, tiled=True)
    slot_count = shard_piece.shape[0]
    group_size, group_count = split_count(slot_count)
    rows_part = tile_row.reshape(group_count, group_size)
    cols_part = tile_col.reshape(group_count, group_size)

    def add_one_turn(running, parts):
        tile_block, rows_sel, cols_sel = parts
        inputs = jnp.take(panel_tiles, cols_sel, axis=1)
        product = jnp.einsum("rsj,sij->rsi", inputs, tile_block, preferred_element_type=jnp.float32)
        placement = (rows_sel[:, None] == row_ids[None, :]).astype(jnp.float32)
        return (
            running
            + jnp.einsum("rsi,sb->rbi", product, placement, precision=lax.Precision.HIGHEST),
            None,
        )

    running_sum, _ = lax.scan(
        add_one_turn,
        running_sum,
        (shard_piece.reshape(group_count, group_size, BLK, BLK), rows_part, cols_part),
    )
    d_hidden = running_sum.reshape(rows_all, row_blocks * BLK)
    d_up = (d_hidden * gate_value * sigmoid_gate).astype(jnp.bfloat16)
    d_gate = (
        d_hidden * up_value * sigmoid_gate * (1.0 + gate_value * (1.0 - sigmoid_gate))
    ).astype(jnp.bfloat16)
    slot_count = fsdp_count * CAP
    group_size, group_count = split_count(slot_count)
    rows_part = tile_row.reshape(group_count, group_size)
    cols_part = tile_col.reshape(group_count, group_size)
    live_part = tile_live.reshape(group_count, group_size)

    def slot_one_turn(parts):
        rows_sel, cols_sel, live_sel = parts
        left_tiles = jnp.take(hidden_tiles, rows_sel, axis=1)
        right_tiles = jnp.take(panel_tiles, cols_sel, axis=1)
        slot_term = jnp.einsum(
            "rsi,rsj->sij", left_tiles, right_tiles, preferred_element_type=jnp.float32
        )
        return slot_term * (grad_scale * live_sel)[:, None, None]

    own_sums = lax.psum_scatter(
        lax.map(slot_one_turn, (rows_part, cols_part, live_part))
        .reshape(slot_count, BLK, BLK)
        .astype(jnp.bfloat16),
        "fsdp",
        scatter_dimension=0,
        tiled=True,
    ).astype(jnp.float32)
    dense_tiles = jnp.einsum(
        "sb,sij->bij", own_choice.astype(jnp.float32), own_sums, precision=lax.Precision.HIGHEST
    )
    d_weight = dense_tiles.reshape(row_blocks, col_blocks, BLK, BLK).transpose(0, 2, 1, 3)
    d_weight = d_weight.reshape(row_blocks * BLK, col_blocks * BLK).astype(jnp.bfloat16)
    return (d_gate, d_up, d_weight)


def solution(mesh):
    return jax.shard_map(
        per_device,
        mesh=mesh,
        in_specs=(
            P(("fsdp", "tensor"), None),
            P(("fsdp", "tensor")),
            P("fsdp", "tensor"),
            P("fsdp", "tensor"),
            P("tensor", "fsdp"),
            P("tensor", None),
        ),
        out_specs=(P("fsdp", "tensor"), P("fsdp", "tensor"), P("tensor", "fsdp")),
        check_vma=False,
    )
```

profile of v0, /device:TPU:16, one launch (start us, length us, event | category | flops | bytes accessed | tf_op | source)
XLA Modules:
  0.0 382.2 jit_solution(10613646936179450982)
XLA Ops:
  15.0 74.8 %all-gather.5.cloned.1.call-done = bf16[128,8192]{1,0:T(8,128)(2,1)} async-done(((bf16[8,8192]{1,0:T(8,128)(2,1)}), bf16[128,8192]{1,0:T(8,128)(2,1)}) %all-gather.5.cloned.1.call-update) | async-done | bytes 2097168 | tf_op jit(solution)/shard_map/all_gather | solution.py:25
  89.8 3.2 copy.64
  93.0 2.9 copy.65
  95.9 84.9 %all-gather.3.cloned.1.call-done = bf16[128,128,128]{2,1,0:T(8,128)(2,1)} async-done(((bf16[4,128,128]{2,1,0:T(8,128)(2,1)}), bf16[128,128,128]{2,1,0:T(8,128)(2,1)}) %all-gather.3.cloned.1.call-update) | async-done | bytes 4194320 | tf_op jit(solution)/shard_map/all_gather | solution.py:64
  180.9 36.9 %while.22 = (s32[]{:T(128)}, f32[128,6,128]{2,1,0:T(8,128)S(1)}, s32[4,32]{1,0:T(4,128)S(1)}, bf16[4,32,128,128]{3,2,1,0:T(8,128)(2,1)}, s32[4,32]{1,0:T(4,128)S...) while((s32[]{:T(128)}, f32[128,6,128]{2,1,0:T(8,128)S(1)}, s32[4,32]{1,0:T(4,128)S(1)}, ...), condition=%wide.region_3.5_spmd.clone, body=%wide.region_2.4_spmd.clone.sunk | while | flops 172688768 | bytes 13374515 | solution.py:81
  180.9 2.3 gather_fusion.2
  183.3 3.5 convolution_bitcast_fusion.3
  186.8 2.4 copy.93
  190.2 2.3 gather_fusion.2
  192.5 3.5 convolution_bitcast_fusion.3
  196.0 2.4 copy.93
  199.4 2.3 gather_fusion.2
  201.7 3.5 convolution_bitcast_fusion.3
  205.2 2.4 copy.93
  208.6 2.3 gather_fusion.2
  211.0 3.5 convolution_bitcast_fusion.3
  214.5 2.4 copy.93
  218.5 19.4 %while.21 = (s32[]{:T(128)}, bf16[4,32,128,128]{3,2,1,0:T(8,128)(2,1)}, s32[4,32]{1,0:T(4,128)S(1)}, bf16[128,6,128]{2,0,1:T(8,128)(2,1)S(1)}, s32[4,32]{1,0:T(4...) while((s32[]{:T(128)}, bf16[4,32,128,128]{3,2,1,0:T(8,128)(2,1)}, ...), condition=%wide.region_6.8_spmd, body=%wide.region_5.7_spmd.sunk | while | flops 135793152 | bytes 8398573 | solution.py:107
  219.3 2.3 gather_fusion
  224.1 2.3 gather_fusion
  226.5 1.7 bitcast_dynamic-update-slice_fusion.2
  229.0 2.3 gather_fusion
  233.8 2.3 gather_fusion
  239.7 133.2 %reduce-scatter.2.cloned.1.call-done = bf16[4,128,128]{2,1,0:T(8,128)(2,1)} async-done(((bf16[128,128,128]{2,1,0:T(8,128)(2,1)}), bf16[4,128,128]{2,1,0:T(8,128)(2,1)}) %reduce-scatter.2.cloned.1.call-update) | async-done | bytes 131088 | tf_op jit(solution)/shard_map/reduce_scatter | solution.py:106
  (91 shorter events, 24.2 us)
Async XLA Ops:
  7.2 7.4 %copy-start = (bf16[128,768]{1,0:T(8,128)(2,1)S(1)}, bf16[128,768]{1,0:T(8,128)(2,1)}, u32[]{:S(2)}) copy-start(bf16[128,768]{1,0:T(8,128)(2,1)} %param.14) | copy-start | bytes 589828
  7.2 7.6 %copy-start.1 = (bf16[128,768]{1,0:T(8,128)(2,1)S(1)}, bf16[128,768]{1,0:T(8,128)(2,1)}, u32[]{:S(2)}) copy-start(bf16[128,768]{1,0:T(8,128)(2,1)} %param.15) | copy-start | bytes 589828
  7.2 82.6 %all-gather.5.cloned.1.call-start = ((), (), s32[]{:S(2)}) async-start(), calls=%async_computation.2 | async-start | bytes 2228224 | tf_op jit(solution)/shard_map/all_gather | solution.py:25
  9.6 171.3 %all-gather.3.cloned.1.call-start = ((), (), s32[]{:S(2)}) async-start(), calls=%async_computation.1 | async-start | bytes 4325376 | tf_op jit(solution)/shard_map/all_gather | solution.py:64
  13.0 359.9 %reduce-scatter.2.cloned.1.call-start = ((), (), s32[]{:S(2)}) async-start(), calls=%async_computation.3 | async-start | bytes 4325376 | tf_op jit(solution)/shard_map/reduce_scatter | solution.py:106
Sparse Core Ops, SparseCore 0:
  10.6 79.0 all-gather.4
  93.7 87.1 all-gather.2
  238.0 134.8 reduce-scatter.1
where the time goes:
time: 383 us; the launch traced here: 382 us
  waiting for transfers between devices  293 us (77%)
  local copies, waits for them, and re-layouts  44.3 us (12%)
  matrix products  26.3 us (7%)
  between operations  14.6 us (4%)
    reduce_scatter x1, waiting for transfers between devices, per_device(): lax.psum_scatter(lax.map(slot_one_turn, (rows_part, cols_part, live_part)...  133 us
    all_gather x1, waiting for transfers between devices, per_device(): shard_piece = lax.all_gather(packed, 'fsdp', axis=0, tiled=True)  84.9 us
    all_gather x1, waiting for transfers between devices, per_device(): grad_panel = lax.all_gather(masked_grad, 'tensor', axis=0, tiled=True)  74.8 us
    dot_general x4, matrix products, add_one_turn(): jnp.einsum('rsj,sij->rsi', inputs, tile_block, preferred_element_type=jnp...  14 us
    transpose x4, local copies, waits for them, and re-layouts, add_one_turn(): jnp.einsum('rsj,sij->rsi', inputs, tile_block, preferred_element_type=jnp...  9.48 us
    gather x4, local copies, waits for them, and re-layouts, add_one_turn(): inputs = jnp.take(panel_tiles, cols_sel, axis=1)  9.36 us
    gather x4, local copies, waits for them, and re-layouts, slot_one_turn(): right_tiles = jnp.take(panel_tiles, cols_sel, axis=1)  9.36 us
  transfers between devices with their start and end apart: 3, of which 3 were waited for; matrix products, arithmetic and copies ran while one was open for 3% of the time, Pallas kernels for 0%

commit v1 on v0

--- a/solution.py
+++ b/solution.py
@@ -22,7 +22,8 @@
     local_count = row_blocks * col_blocks
     live_mask = jnp.arange(tok_rows)[:, None] < live_rows[0]
     masked_grad = jnp.where(live_mask, out_grad, jnp.zeros_like(out_grad))
-    grad_panel = lax.all_gather(masked_grad, "tensor", axis=0, tiled=True)
+    repeated = jnp.stack([masked_grad] * lax.axis_size("tensor"))
+    grad_panel = jnp.concatenate(lax.all_to_all(repeated, "tensor", 0, 0), axis=0)
     rows_all = grad_panel.shape[0]
     panel_tiles = grad_panel.reshape(rows_all, fsdp_count * col_blocks, BLK)
     shard_masks = (

time: 383 us -> 313 us (0.82)
  waiting for transfers between devices: 293 us -> 214 us
  starting transfers between devices: 0.12 us -> 11.6 us
    all_gather x1 -> x0, waiting for transfers between devices: 74.8 us -> none  [per_device(): grad_panel = lax.all_gather(masked_grad, 'tensor', axis=0, tiled=True)]
    all_gather x1, waiting for transfers between devices: 84.9 us -> 34 us  [per_device(): shard_piece = lax.all_gather(packed, 'fsdp', axis=0, tiled=True)]
    all_to_all x0 -> x1, waiting for transfers between devices: none -> 46.8 us  [per_device(): lax.all_to_all(repeated, 'tensor', 0, 0)]
    all_to_all x0 -> x1, starting transfers between devices: none -> 11.5 us  [per_device(): lax.all_to_all(repeated, 'tensor', 0, 0)]
where the time goes in v1:
time: 313 us; the launch traced here: 312 us
  waiting for transfers between devices  214 us (68%)
  local copies, waits for them, and re-layouts  43.1 us (14%)
  matrix products  26.3 us (8%)
  between operations  14.9 us (5%)
  starting transfers between devices  11.6 us (4%)
    reduce_scatter x1, waiting for transfers between devices, per_device(): lax.psum_scatter(lax.map(slot_one_turn, (rows_part, cols_part, live_part)...  133 us
    all_to_all x1, waiting for transfers between devices, per_device(): lax.all_to_all(repeated, 'tensor', 0, 0)  46.8 us
    all_gather x1, waiting for transfers between devices, per_device(): shard_piece = lax.all_gather(packed, 'fsdp', axis=0, tiled=True)  34 us
    dot_general x4, matrix products, add_one_turn(): jnp.einsum('rsj,sij->rsi', inputs, tile_block, preferred_element_type=jnp...  13.9 us
    all_to_all x1, starting transfers between devices, per_device(): lax.all_to_all(repeated, 'tensor', 0, 0)  11.5 us
    transpose x4, local copies, waits for them, and re-layouts, add_one_turn(): jnp.einsum('rsj,sij->rsi', inputs, tile_block, preferred_element_type=jnp...  9.48 us
    gather x4, local copies, waits for them, and re-layouts, add_one_turn(): inputs = jnp.take(panel_tiles, cols_sel, axis=1)  9.36 us
    gather x4, local copies, waits for them, and re-layouts, slot_one_turn(): right_tiles = jnp.take(panel_tiles, cols_sel, axis=1)  9.36 us
  transfers between devices with their start and end apart: 3, of which 3 were waited for; matrix products, arithmetic and copies ran while one was open for 3% of the time, Pallas kernels for 0%

profile of v1, /device:TPU:16, one launch (start us, length us, event | category | flops | bytes accessed | tf_op | source)
XLA Modules:
  0.0 312.1 jit_solution(5391269633309313420)
XLA Ops:
  12.9 11.5 %all-to-all-start = ((bf16[16,8,8192]{2,1,0:T(8,128)(2,1)}), bf16[16,8,8192]{2,1,0:T(8,128)(2,1)S(1)}, u32[]{:S(2)}, u32[]{:S(2)}) async-start(bf16[16,8,8192]{2,1,0:T(8,128)(2,1)} %stack.2), calls=%async_computation | async-start | bytes 4194304 | tf_op jit(solution)/shard_map/all_to_all | solution.py:26
  26.3 46.8 %all-to-all-done = bf16[16,8,8192]{2,1,0:T(8,128)(2,1)S(1)} async-done(((bf16[16,8,8192]{2,1,0:T(8,128)(2,1)}), bf16[16,8,8192]{2,1,0:T(8,128)(2,1)S(1)}, u32[]{:S(2)}, u32[]{:S(2)}) %all-to-all-start) | async-done | bytes 2097184 | tf_op jit(solution)/shard_map/all_to_all | solution.py:26
  73.8 2.7 copy.63
  76.5 34.0 %all-gather.2.cloned.1.call-done = bf16[128,128,128]{2,1,0:T(8,128)(2,1)} async-done(((bf16[4,128,128]{2,1,0:T(8,128)(2,1)}), bf16[128,128,128]{2,1,0:T(8,128)(2,1)}) %all-gather.2.cloned.1.call-update) | async-done | bytes 4194320 | tf_op jit(solution)/shard_map/all_gather | solution.py:65
  110.5 36.9 %while.22 = (s32[]{:T(128)}, f32[128,6,128]{2,1,0:T(8,128)S(1)}, s32[4,32]{1,0:T(4,128)S(1)}, bf16[4,32,128,128]{3,2,1,0:T(8,128)(2,1)}, s32[4,32]{1,0:T(4,128)S...) while((s32[]{:T(128)}, f32[128,6,128]{2,1,0:T(8,128)S(1)}, s32[4,32]{1,0:T(4,128)S(1)}, ...), condition=%wide.region_3.5_spmd.clone, body=%wide.region_2.4_spmd.clone.sunk | while | flops 172688768 | bytes 13374515 | solution.py:82
  110.5 2.3 gather_fusion.2
  112.9 3.5 %convolution_bitcast_fusion.3 = f32[128,32,128]{0,2,1:T(8,128)} fusion(bf16[32,128,128]{2,1,0:T(8,128)(2,1)S(1)} %gather_fusion.2, bf16[4,32,128,128]{3,2,1,0:T(8,128)(2,1)} %get-tuple-element.304, s32[]{:T(128)S(6)} %copy.96, pred[32]{0:T(512)(128)(4,1)S(1)} %get-tuple-element.284), kind=kOutput, calls=%fused_computation.27.clone.1 | convolution fusion | flops 134742016 | bytes 4194340 | tf_op jit(solution)/shard_map/while/body/eval_jaxpr/rsj,sij->rsi/dot_general | solution.py:74
  116.4 2.4 copy.92
  119.8 2.3 gather_fusion.2
  122.1 3.5 %convolution_bitcast_fusion.3 = f32[128,32,128]{0,2,1:T(8,128)} fusion(bf16[32,128,128]{2,1,0:T(8,128)(2,1)S(1)} %gather_fusion.2, bf16[4,32,128,128]{3,2,1,0:T(8,128)(2,1)} %get-tuple-element.304, s32[]{:T(128)S(6)} %copy.96, pred[32]{0:T(512)(128)(4,1)S(1)} %get-tuple-element.284), kind=kOutput, calls=%fused_computation.27.clone.1 | convolution fusion | flops 134742016 | bytes 4194340 | tf_op jit(solution)/shard_map/while/body/eval_jaxpr/rsj,sij->rsi/dot_general | solution.py:74
  125.6 2.4 copy.92
  129.0 2.3 gather_fusion.2
  131.3 3.5 %convolution_bitcast_fusion.3 = f32[128,32,128]{0,2,1:T(8,128)} fusion(bf16[32,128,128]{2,1,0:T(8,128)(2,1)S(1)} %gather_fusion.2, bf16[4,32,128,128]{3,2,1,0:T(8,128)(2,1)} %get-tuple-element.304, s32[]{:T(128)S(6)} %copy.96, pred[32]{0:T(512)(128)(4,1)S(1)} %get-tuple-element.284), kind=kOutput, calls=%fused_computation.27.clone.1 | convolution fusion | flops 134742016 | bytes 4194340 | tf_op jit(solution)/shard_map/while/body/eval_jaxpr/rsj,sij->rsi/dot_general | solution.py:74
  134.8 2.4 copy.92
  138.2 2.3 gather_fusion.2
  140.6 3.5 %convolution_bitcast_fusion.3 = f32[128,32,128]{0,2,1:T(8,128)} fusion(bf16[32,128,128]{2,1,0:T(8,128)(2,1)S(1)} %gather_fusion.2, bf16[4,32,128,128]{3,2,1,0:T(8,128)(2,1)} %get-tuple-element.304, s32[]{:T(128)S(6)} %copy.96, pred[32]{0:T(512)(128)(4,1)S(1)} %get-tuple-element.284), kind=kOutput, calls=%fused_computation.27.clone.1 | convolution fusion | flops 134742016 | bytes 4194340 | tf_op jit(solution)/shard_map/while/body/eval_jaxpr/rsj,sij->rsi/dot_general | solution.py:74
  144.1 2.4 copy.92
  148.0 19.4 %while.21 = (s32[]{:T(128)}, bf16[4,32,128,128]{3,2,1,0:T(8,128)(2,1)}, s32[4,32]{1,0:T(4,128)S(1)}, bf16[128,6,128]{2,0,1:T(8,128)(2,1)S(1)}, s32[4,32]{1,0:T(4...) while((s32[]{:T(128)}, bf16[4,32,128,128]{3,2,1,0:T(8,128)(2,1)}, ...), condition=%wide.region_6.8_spmd, body=%wide.region_5.7_spmd.sunk | while | flops 135793152 | bytes 8398573 | solution.py:108
  148.9 2.3 gather_fusion
  153.7 2.3 gather_fusion
  158.5 2.3 gather_fusion
  163.4 2.3 gather_fusion
  165.7 1.7 bitcast_dynamic-update-slice_fusion.2
  169.3 133.2 %reduce-scatter.2.cloned.1.call-done = bf16[4,128,128]{2,1,0:T(8,128)(2,1)} async-done(((bf16[128,128,128]{2,1,0:T(8,128)(2,1)}), bf16[4,128,128]{2,1,0:T(8,128)(2,1)}) %reduce-scatter.2.cloned.1.call-update) | async-done | bytes 131088 | tf_op jit(solution)/shard_map/reduce_scatter | solution.py:107
  (93 shorter events, 24.8 us)
Async XLA Ops:
  7.2 4.1 %copy-start.2 = (bf16[8,8192]{1,0:T(8,128)(2,1)S(1)}, bf16[8,8192]{1,0:T(8,128)(2,1)}, u32[]{:S(2)}) copy-start(bf16[8,8192]{1,0:T(8,128)(2,1)} %param.12) | copy-start | bytes 393220
  7.2 103.3 %all-gather.2.cloned.1.call-start = ((), (), s32[]{:S(2)}) async-start(), calls=%async_computation.2 | async-start | bytes 4325376 | tf_op jit(solution)/shard_map/all_gather | solution.py:65
  12.9 13.1 %copy-start = (bf16[128,768]{1,0:T(8,128)(2,1)S(1)}, bf16[128,768]{1,0:T(8,128)(2,1)}, u32[]{:S(2)}) copy-start(bf16[128,768]{1,0:T(8,128)(2,1)} %param.14) | copy-start | bytes 589828
  12.9 13.2 %copy-start.1 = (bf16[128,768]{1,0:T(8,128)(2,1)S(1)}, bf16[128,768]{1,0:T(8,128)(2,1)}, u32[]{:S(2)}) copy-start(bf16[128,768]{1,0:T(8,128)(2,1)} %param.15) | copy-start | bytes 589828
  12.9 60.2 %all-to-all-start = ((bf16[16,8,8192]{2,1,0:T(8,128)(2,1)}), bf16[16,8,8192]{2,1,0:T(8,128)(2,1)S(1)}, u32[]{:S(2)}, u32[]{:S(2)}) async-start(bf16[16,8,8192]{2,1,0:T(8,128)(2,1)} %stack.2), calls=%async_computation | async-start | bytes 4194304 | tf_op jit(solution)/shard_map/all_to_all | solution.py:26
  24.4 278.1 %reduce-scatter.2.cloned.1.call-start = ((), (), s32[]{:S(2)}) async-start(), calls=%async_computation.3 | async-start | bytes 4325376 | tf_op jit(solution)/shard_map/reduce_scatter | solution.py:107
Sparse Core Ops, SparseCore 0:
  11.9 98.5 all-gather.1
  167.6 134.8 reduce-scatter.1
